TPU v7x, 32 devices: a whole 2x2x4 slice. The times are simulated.
32 devices in a mesh: row: 8 (over z, x), col: 4 (over y, core).
Axes of the slice: x: 2, y: 2, z: 4, core: 2. Of those that a mesh axis runs over, the one named last changes fastest.
Arguments:
- affinity: bfloat16 [32768, 8192], P('row', 'col'), may hold values from -250 to 250
- seed_values: int32 [16], replicated, may hold values from 0 to 1073741823
- sku_ids: int32 [8192], P('col'), may hold values from 0 to 8191, each once
Outputs:
- range_basis: float32 [16, 32768], P(None, ('row', 'col'))
- range_factor: float32 [16, 16], replicated
All inputs are finite; a program needn't handle non-finite values.
Results may differ from a plain program's by a relative error of at most 0.0046.
Values may be sent and summed in bfloat16 or wider, within the bound.
A program may use at most 64 MiB of HBM per device.

v0:
```python
import math
import jax
import jax.numpy as jnp
from jax import lax
from jax.sharding import PartitionSpec as P

ITERS = 2
mix_first = -2048144789
mix_second = -1028477387
golden = -1640531535
salt_value = 1540483477


def shifted(value, amount):
    return lax.shift_right_logical(value, jnp.full(value.shape, amount, jnp.int32))


def scramble(value):
    value = jnp.bitwise_xor(value, shifted(value, 16))
    value = value * jnp.int32(mix_first)
    value = jnp.bitwise_xor(value, shifted(value, 13))
    value = value * jnp.int32(mix_second)
    return jnp.bitwise_xor(value, shifted(value, 16))


def test_matrix(seed_values, sku_ids, total_columns):
    first = scramble(jnp.bitwise_xor(seed_values[:, None], sku_ids[None, :] * jnp.int32(golden)))
    second = scramble(jnp.bitwise_xor(first, jnp.int32(salt_value)))
    uniform_a = (shifted(first, 9) + 1).astype(jnp.float32) / 8388608.0
    uniform_b = (shifted(second, 9) + 1).astype(jnp.float32) / 8388608.0
    gauss = jnp.sqrt(-2.0 * jnp.log(uniform_a)) * jnp.cos(6.283185307179586 * uniform_b)
    return (gauss / math.sqrt(total_columns)).astype(jnp.bfloat16)


def lower_solve(lower, right):
    return lax.linalg.triangular_solve(lower, right, left_side=True, lower=True)


def body(affinity, seed_values, sku_ids):
    col_count = lax.axis_size("col")
    total_columns = sku_ids.shape[0] * col_count
    local_rows = affinity.shape[0]
    piece_rows = local_rows // col_count
    total_rows = local_rows * lax.axis_size("row")
    inv_root = 1.0 / math.sqrt(total_columns)

    def project(left):
        return lax.dot_general(
            left, affinity, (((1,), (1,)), ((), ())), preferred_element_type=jnp.float32
        )

    omega = test_matrix(seed_values, sku_ids, total_columns)
    partial_sketch = project(omega)
    for repeat in range(ITERS + 1):
        sketch = lax.psum(partial_sketch, "col")
        gram = lax.psum(
            jnp.dot(
                sketch,
                sketch.T,
                precision=lax.Precision.HIGHEST,
                preferred_element_type=jnp.float32,
            ),
            "row",
        )
        lower = jnp.linalg.cholesky(gram)
        ortho = lower_solve(lower, sketch)
        if repeat < ITERS:
            back_part = jnp.dot(
                ortho.astype(jnp.bfloat16), affinity, preferred_element_type=jnp.float32
            )
        else:
            start_row = lax.axis_index("col") * piece_rows
            ortho = lax.dynamic_slice_in_dim(ortho, start_row, piece_rows, 1)
        if repeat < ITERS:
            back = lax.psum(back_part, "row")
            partial_sketch = project(back.astype(jnp.bfloat16)) * inv_root
    scale = math.sqrt(total_rows)
    return (ortho * scale, lower.T / scale)


def solution(mesh):
    placed = (P("row", "col"), P(), P("col"))
    return jax.shard_map(
        body, mesh=mesh, in_specs=placed, out_specs=(P(None, ("row", "col")), P()), check_vma=False
    )
```

profile of v0, /device:TPU:0, one launch (start us, length us, event | category | flops | bytes accessed | tf_op | source)
XLA Modules:
  0.0 315.6 jit_solution(10747152659197352157)
XLA Ops:
  7.2 0.0 all-reduce.6.cloned.1.call-start
  7.2 0.7 broadcast_multiply_fusion
  7.9 11.5 %fusion.12 = f32[16,4096]{1,0:T(8,128)} fusion(bf16[4096,2048]{1,0:T(8,128)(2,1)} %param.6, s32[2048]{0:T(1024)S(1)} %broadcast_multiply_fusion, s32[16]{0:T(128)} %param.7), kind=kOutput, calls=%fused_computation.22 | convolution fusion | flops 269418496 | bytes 17047616 | tf_op jit(solution)/shard_map/dot_general | solution.py:48
  19.5 0.0 all-reduce.6.cloned.1.call-update
  19.5 0.0 all-reduce.8.cloned.1.call-start
  19.5 35.1 %all-reduce.6.cloned.1.call-done = f32[16,4096]{1,0:T(8,128)} async-done(((f32[16,4096]{1,0:T(8,128)}), f32[16,4096]{1,0:T(8,128)}) %all-reduce.6.cloned.1.call-update) | async-done | bytes 262160 | tf_op jit(solution)/shard_map/psum | solution.py:55
  54.6 1.5 fusion.54
  56.1 21.6 %psum.57 = f32[16,16]{0,1:T(8,128)S(1)} all-reduce(f32[16,16]{0,1:T(8,128)S(1)} %fusion.54), channel_id=1, replica_groups=mesh['row'=8,'col'=4] {'row'}, use_global_device_ids=true, to_apply=%region_1.0 | all-reduce | flops 256 | bytes 2048 | tf_op jit(solution)/shard_map/psum | solution.py:56
  77.7 0.1 copy.6
  77.8 1.5 cholesky.59
  79.3 0.6 compare_reduce_fusion.2
  79.9 0.6 fusion.29
  80.6 1.2 custom-call.7
  81.8 1.4 convolution_convert_fusion.1
  83.2 8.0 %fusion.55 = f32[16,2048]{1,0:T(8,128)S(1)} fusion(bf16[16,4096]{1,0:T(8,128)(2,1)S(1)} %convolution_convert_fusion.1, bf16[4096,2048]{1,0:T(8,128)(2,1)} %param.6), kind=kOutput, calls=%fused_computation.79 | convolution fusion | flops 268435456 | bytes 17039360 | tf_op jit(solution)/shard_map/dot_general | solution.py:68
  91.3 34.2 %all-reduce.11 = bf16[16,2048]{1,0:T(8,128)(2,1)S(1)} all-reduce(f32[16,2048]{1,0:T(8,128)S(1)} %fusion.55), channel_id=1, replica_groups=mesh['row'=8,'col'=4] {'row'}, use_global_device_ids=true, to_apply=%region_4.7 | all-reduce | flops 32768 | bytes 196608 | tf_op jit(solution)/shard_map/psum | solution.py:75
  125.5 10.9 %convolution_multiply_fusion.1 = f32[16,4096]{1,0:T(8,128)} fusion(bf16[4096,2048]{1,0:T(8,128)(2,1)} %param.6, bf16[16,2048]{1,0:T(8,128)(2,1)S(1)} %all-reduce.11), kind=kOutput, calls=%fused_computation.1 | convolution fusion | flops 268500992 | bytes 17104896 | tf_op jit(solution)/shard_map/dot_general | solution.py:48
  136.4 0.0 all-reduce.8.cloned.1.call-update
  136.4 0.0 all-reduce.10.cloned.1.call-start
  136.5 30.3 %all-reduce.8.cloned.1.call-done = f32[16,4096]{1,0:T(8,128)} async-done(((f32[16,4096]{1,0:T(8,128)}), f32[16,4096]{1,0:T(8,128)}) %all-reduce.8.cloned.1.call-update) | async-done | bytes 262160 | tf_op jit(solution)/shard_map/psum | solution.py:55
  166.8 1.5 fusion.56
  168.3 21.8 %psum.60 = f32[16,16]{0,1:T(8,128)S(1)} all-reduce(f32[16,16]{0,1:T(8,128)S(1)} %fusion.56), channel_id=1, replica_groups=mesh['row'=8,'col'=4] {'row'}, use_global_device_ids=true, to_apply=%region_6.9 | all-reduce | flops 256 | bytes 2048 | tf_op jit(solution)/shard_map/psum | solution.py:56
  190.1 0.1 copy.8
  190.2 1.5 cholesky.70
  191.6 0.6 compare_reduce_fusion.1
  192.3 0.6 fusion.30
  192.9 1.2 custom-call.8
  194.2 1.4 convolution_convert_fusion
  195.6 8.0 %fusion.57 = f32[16,2048]{1,0:T(8,128)S(1)} fusion(bf16[16,4096]{1,0:T(8,128)(2,1)S(1)} %convolution_convert_fusion, bf16[4096,2048]{1,0:T(8,128)(2,1)} %param.6), kind=kOutput, calls=%fused_computation.81 | convolution fusion | flops 268435456 | bytes 17039360 | tf_op jit(solution)/shard_map/dot_general | solution.py:68
  203.6 34.2 %all-reduce.12 = bf16[16,2048]{1,0:T(8,128)(2,1)S(1)} all-reduce(f32[16,2048]{1,0:T(8,128)S(1)} %fusion.57), channel_id=1, replica_groups=mesh['row'=8,'col'=4] {'row'}, use_global_device_ids=true, to_apply=%region_7.10 | all-reduce | flops 32768 | bytes 196608 | tf_op jit(solution)/shard_map/psum | solution.py:75
  237.8 10.9 %convolution_multiply_fusion = f32[16,4096]{1,0:T(8,128)} fusion(bf16[4096,2048]{1,0:T(8,128)(2,1)} %param.6, bf16[16,2048]{1,0:T(8,128)(2,1)S(1)} %all-reduce.12), kind=kOutput, calls=%fused_computation | convolution fusion | flops 268500992 | bytes 17104896 | tf_op jit(solution)/shard_map/dot_general | solution.py:48
  248.7 0.0 all-reduce.10.cloned.1.call-update
  248.8 30.4 %all-reduce.10.cloned.1.call-done = f32[16,4096]{1,0:T(8,128)} async-done(((f32[16,4096]{1,0:T(8,128)}), f32[16,4096]{1,0:T(8,128)}) %all-reduce.10.cloned.1.call-update) | async-done | bytes 262160 | tf_op jit(solution)/shard_map/psum | solution.py:55
  279.2 1.5 fusion.58
  280.6 21.6 %psum.63 = f32[16,16]{0,1:T(8,128)S(1)} all-reduce(f32[16,16]{0,1:T(8,128)S(1)} %fusion.58), channel_id=1, replica_groups=mesh['row'=8,'col'=4] {'row'}, use_global_device_ids=true, to_apply=%region_9.12 | all-reduce | flops 256 | bytes 2048 | tf_op jit(solution)/shard_map/psum | solution.py:56
  302.3 0.1 copy.10
  302.3 1.5 cholesky.81
  303.8 0.6 compare_reduce_fusion
  304.5 0.7 multiply_bitcast_fusion
  305.1 1.2 custom-call.9
  306.4 0.7 copy.11
  307.0 1.4 fusion.31
  308.4 0.6 dynamic-slice_multiply_fusion
  (6 shorter events, 0.1 us)
Async XLA Ops:
  7.2 47.5 %all-reduce.6.cloned.1.call-start = ((), (), s32[]{:S(2)}) async-start(), calls=%async_computation | async-start | bytes 524288 | tf_op jit(solution)/shard_map/psum | solution.py:55
  19.5 147.3 %all-reduce.8.cloned.1.call-start = ((), (), s32[]{:S(2)}) async-start(), calls=%async_computation.1 | async-start | bytes 524288 | tf_op jit(solution)/shard_map/psum | solution.py:55
  136.4 142.8 %all-reduce.10.cloned.1.call-start = ((), (), s32[]{:S(2)}) async-start(), calls=%async_computation.2 | async-start | bytes 524288 | tf_op jit(solution)/shard_map/psum | solution.py:55
Sparse Core Ops, SparseCore 0:
  19.6 34.9 all-reduce.5
  136.5 30.2 all-reduce.7
  248.9 30.2 all-reduce.9
where the time goes:
time: 316 us
  blocking collectives  133 us (42%)
  waiting for transfers between devices  95.9 us (30%)
  matrix products  58 us (18%)
  between operations  13.8 us (4%)
  other arithmetic  13.4 us (4%)
    psum x3, waiting for transfers between devices, body(): sketch = lax.psum(partial_sketch, 'col')  95.9 us
    psum x2, blocking collectives, body(): back = lax.psum(back_part, 'row')  68.4 us
    psum x3, blocking collectives, body(): lax.psum(jnp.dot(sketch, sketch.T, precision=lax.Precision.HIGHEST, prefe...  65 us
    dot_general x3, matrix products, project(): lax.dot_general(left, affinity, (((1,), (1,)), ((), ())), preferred_eleme...  33.4 us
    dot_general x2, matrix products, body(): jnp.dot(ortho.astype(jnp.bfloat16), affinity, preferred_element_type=jnp....  16.1 us
    another operation x9, other arithmetic, body(): lower = jnp.linalg.cholesky(gram)  6.39 us
  transfers between devices with their start and end apart: 3, of which 3 were waited for; matrix products, arithmetic and copies ran while one was open for 0% of the time, Pallas kernels for 0%

commit v1 on v0

--- a/solution.py
+++ b/solution.py
@@ -52,7 +52,12 @@
     omega = test_matrix(seed_values, sku_ids, total_columns)
     partial_sketch = project(omega)
     for repeat in range(ITERS + 1):
-        sketch = lax.psum(partial_sketch, "col")
+        sketch = partial_sketch
+        n_all = lax.axis_size("col")
+        for kk in [
+            [(to_i, to_i ^ p) for to_i in range(n_all)] for p in (1, 2, 4, 8, 16) if p < n_all
+        ]:
+            sketch = sketch + lax.ppermute(sketch, "col", kk)
         gram = lax.psum(
             jnp.dot(
                 sketch,

time: 316 us -> 227 us (0.72)
  waiting for transfers between devices: 95.9 us -> 24.5 us
  between operations: 13.8 us -> 0.75 us
  matrix products: 58 us -> 50 us
  starting transfers between devices: 0.12 us -> 6.63 us
    psum x3 -> x0, waiting for transfers between devices: 95.9 us -> none  [body(): sketch = lax.psum(partial_sketch, 'col')]
    ppermute x0 -> x6, waiting for transfers between devices: none -> 24.5 us  [body(): sketch = sketch + lax.ppermute(sketch, 'col', kk)]
    ppermute x0 -> x6, starting transfers between devices: none -> 6.63 us  [body(): sketch = sketch + lax.ppermute(sketch, 'col', kk)]
    psum x3, blocking collectives: 65 us -> 61.5 us  [body(): lax.psum(jnp.dot(sketch, sketch.T, precision=lax.Precision.HIGHEST, prefe...]
  transfers between devices with their start and end apart: 3 -> 6, of which waited for: 3 -> 6; matrix products, arithmetic and copies ran while one was open for 0% -> 0% of each run, Pallas kernels for 0% -> 0%
where the time goes in v1:
time: 227 us; the launch traced here: 226 us
  blocking collectives  130 us (57%)
  matrix products  50 us (22%)
  waiting for transfers between devices  24.5 us (11%)
  other arithmetic  13.6 us (6%)
  starting transfers between devices  6.63 us (3%)
    psum x2, blocking collectives, body(): back = lax.psum(back_part, 'row')  68.4 us
    psum x3, blocking collectives, body(): lax.psum(jnp.dot(sketch, sketch.T, precision=lax.Precision.HIGHEST, prefe...  61.5 us
    dot_general x3, matrix products, project(): lax.dot_general(left, affinity, (((1,), (1,)), ((), ())), preferred_eleme...  31.2 us
    ppermute x6, waiting for transfers between devices, body(): sketch = sketch + lax.ppermute(sketch, 'col', kk)  24.5 us
    dot_general x2, matrix products, body(): jnp.dot(ortho.astype(jnp.bfloat16), affinity, preferred_element_type=jnp....  16.1 us
    ppermute x6, starting transfers between devices, body(): sketch = sketch + lax.ppermute(sketch, 'col', kk)  6.63 us
    another operation x9, other arithmetic, body(): lower = jnp.linalg.cholesky(gram)  6.39 us
    another operation x5, other arithmetic, lower_solve(): return lax.linalg.triangular_solve(lower, right, left_side=True, lower=True)  4.98 us
  transfers between devices with their start and end apart: 6, of which 6 were waited for; matrix products, arithmetic and copies ran while one was open for 0% of the time, Pallas kernels for 0%

profile of v1, /device:TPU:0, one launch (start us, length us, event | category | flops | bytes accessed | tf_op | source)
XLA Modules:
  0.0 226.3 jit_solution(201377899414715962)
XLA Ops:
  0.6 0.7 broadcast_multiply_fusion
  1.3 10.8 %fusion.12 = f32[16,4096]{1,0:T(8,128)S(1)} fusion(bf16[4096,2048]{1,0:T(8,128)(2,1)} %param.6, s32[2048]{0:T(1024)S(1)} %broadcast_multiply_fusion, s32[16]{0:T(128)} %param.7), kind=kOutput, calls=%fused_computation.22 | convolution fusion | flops 269418496 | bytes 17047616 | tf_op jit(solution)/shard_map/dot_general | solution.py:48
  12.2 0.5 collective-permute-start
  12.7 1.2 collective-permute-done
  13.9 2.9 %collective-permute-start.1 = (f32[16,4096]{1,0:T(8,128)S(1)}, f32[16,4096]{1,0:T(8,128)S(1)}, u32[]{:S(2)}, u32[]{:S(2)}) collective-permute-start(f32[16,4096]{1,0:T(8,128)S(1)} %add.47), channel_id=1, source_target_pairs={{0,2},{1,3},{2,0},{3,1},{4,6},{5,7},{6,4},{7,5},{8,10},{9,11},{10,... | collective-permute-start | bytes 786440 | tf_op jit(solution)/shard_map/ppermute | solution.py:60
  16.8 6.6 %collective-permute-done.1 = f32[16,4096]{1,0:T(8,128)S(1)} collective-permute-done((f32[16,4096]{1,0:T(8,128)S(1)}, f32[16,4096]{1,0:T(8,128)S(1)}, u32[]{:S(2)}, u32[]{:S(2)}) %collective-permute-start.1) | collective-permute-done | bytes 262176 | tf_op jit(solution)/shard_map/ppermute | solution.py:60
  23.4 0.5 fusion.54
  23.9 22.1 %psum.35 = f32[16,16]{0,1:T(8,128)S(1)} all-reduce(f32[16,16]{0,1:T(8,128)S(1)} %fusion.54), channel_id=1, replica_groups=mesh['row'=8,'col'=4] {'row'}, use_global_device_ids=true, to_apply=%region_0.0 | all-reduce | flops 256 | bytes 2048 | tf_op jit(solution)/shard_map/psum | solution.py:61
  46.0 0.1 copy.6
  46.1 1.5 cholesky.59
  47.6 0.6 compare_reduce_fusion.2
  48.2 0.6 fusion.29
  48.9 1.2 custom-call.7
  50.1 0.4 convolution_convert_fusion.1
  50.6 8.0 %fusion.55 = f32[16,2048]{1,0:T(8,128)S(1)} fusion(bf16[16,4096]{1,0:T(8,128)(2,1)S(1)} %convolution_convert_fusion.1, bf16[4096,2048]{1,0:T(8,128)(2,1)} %param.6), kind=kOutput, calls=%fused_computation.79 | convolution fusion | flops 268435456 | bytes 17039360 | tf_op jit(solution)/shard_map/dot_general | solution.py:73
  58.6 34.2 %all-reduce.2 = bf16[16,2048]{1,0:T(8,128)(2,1)S(1)} all-reduce(f32[16,2048]{1,0:T(8,128)S(1)} %fusion.55), channel_id=1, replica_groups=mesh['row'=8,'col'=4] {'row'}, use_global_device_ids=true, to_apply=%region_3.6 | all-reduce | flops 32768 | bytes 196608 | tf_op jit(solution)/shard_map/psum | solution.py:80
  92.8 10.2 %convolution_multiply_fusion.1 = f32[16,4096]{1,0:T(8,128)S(1)} fusion(bf16[4096,2048]{1,0:T(8,128)(2,1)} %param.6, bf16[16,2048]{1,0:T(8,128)(2,1)S(1)} %all-reduce.2), kind=kOutput, calls=%fused_computation.1 | convolution fusion | flops 268500992 | bytes 17104896 | tf_op jit(solution)/shard_map/dot_general | solution.py:48
  103.0 0.0 collective-permute-start.2
  103.0 1.5 collective-permute-done.2
  104.6 1.6 collective-permute-start.3
  106.2 6.8 %collective-permute-done.3 = f32[16,4096]{1,0:T(8,128)S(1)} collective-permute-done((f32[16,4096]{1,0:T(8,128)S(1)}, f32[16,4096]{1,0:T(8,128)S(1)}, u32[]{:S(2)}, u32[]{:S(2)}) %collective-permute-start.3) | collective-permute-done | bytes 262176 | tf_op jit(solution)/shard_map/ppermute | solution.py:60
  113.0 0.5 fusion.56
  113.5 19.8 %psum.37 = f32[16,16]{0,1:T(8,128)S(1)} all-reduce(f32[16,16]{0,1:T(8,128)S(1)} %fusion.56), channel_id=1, replica_groups=mesh['row'=8,'col'=4] {'row'}, use_global_device_ids=true, to_apply=%region_4.7 | all-reduce | flops 256 | bytes 2048 | tf_op jit(solution)/shard_map/psum | solution.py:61
  133.3 0.1 copy.8
  133.4 1.5 cholesky.70
  134.9 0.6 compare_reduce_fusion.1
  135.5 0.6 fusion.30
  136.2 1.2 custom-call.8
  137.4 0.4 convolution_convert_fusion
  137.9 8.0 %fusion.57 = f32[16,2048]{1,0:T(8,128)S(1)} fusion(bf16[16,4096]{1,0:T(8,128)(2,1)S(1)} %convolution_convert_fusion, bf16[4096,2048]{1,0:T(8,128)(2,1)} %param.6), kind=kOutput, calls=%fused_computation.81 | convolution fusion | flops 268435456 | bytes 17039360 | tf_op jit(solution)/shard_map/dot_general | solution.py:73
  145.9 34.3 %all-reduce.3 = bf16[16,2048]{1,0:T(8,128)(2,1)S(1)} all-reduce(f32[16,2048]{1,0:T(8,128)S(1)} %fusion.57), channel_id=1, replica_groups=mesh['row'=8,'col'=4] {'row'}, use_global_device_ids=true, to_apply=%region_5.8 | all-reduce | flops 32768 | bytes 196608 | tf_op jit(solution)/shard_map/psum | solution.py:80
  180.2 10.2 %convolution_multiply_fusion = f32[16,4096]{1,0:T(8,128)S(1)} fusion(bf16[4096,2048]{1,0:T(8,128)(2,1)} %param.6, bf16[16,2048]{1,0:T(8,128)(2,1)S(1)} %all-reduce.3), kind=kOutput, calls=%fused_computation | convolution fusion | flops 268500992 | bytes 17104896 | tf_op jit(solution)/shard_map/dot_general | solution.py:48
  190.4 0.0 collective-permute-start.4
  190.4 1.5 collective-permute-done.4
  191.9 1.6 collective-permute-start.5
  193.5 6.8 %collective-permute-done.5 = f32[16,4096]{1,0:T(8,128)S(1)} collective-permute-done((f32[16,4096]{1,0:T(8,128)S(1)}, f32[16,4096]{1,0:T(8,128)S(1)}, u32[]{:S(2)}, u32[]{:S(2)}) %collective-permute-start.5) | collective-permute-done | bytes 262176 | tf_op jit(solution)/shard_map/ppermute | solution.py:60
  200.4 0.5 fusion.58
  200.9 19.6 %psum.39 = f32[16,16]{0,1:T(8,128)S(1)} all-reduce(f32[16,16]{0,1:T(8,128)S(1)} %fusion.58), channel_id=1, replica_groups=mesh['row'=8,'col'=4] {'row'}, use_global_device_ids=true, to_apply=%region_6.9 | all-reduce | flops 256 | bytes 2048 | tf_op jit(solution)/shard_map/psum | solution.py:61
  220.4 0.1 copy.10
  220.5 1.5 cholesky.81
  222.0 0.6 compare_reduce_fusion
  222.6 0.7 multiply_bitcast_fusion
  223.3 1.2 custom-call.9
  224.5 0.4 fusion.31
  225.0 0.7 copy.11
  225.6 0.6 dynamic-slice_multiply_fusion
  (12 shorter events, 0.3 us)
Async XLA Ops:
  12.2 1.7 collective-permute-start
  13.9 9.5 %collective-permute-start.1 = (f32[16,4096]{1,0:T(8,128)S(1)}, f32[16,4096]{1,0:T(8,128)S(1)}, u32[]{:S(2)}, u32[]{:S(2)}) collective-permute-start(f32[16,4096]{1,0:T(8,128)S(1)} %add.47), channel_id=1, source_target_pairs={{0,2},{1,3},{2,0},{3,1},{4,6},{5,7},{6,4},{7,5},{8,10},{9,11},{10,... | collective-permute-start | bytes 786440 | tf_op jit(solution)/shard_map/ppermute | solution.py:60
  103.0 1.6 collective-permute-start.2
  104.6 8.4 %collective-permute-start.3 = (f32[16,4096]{1,0:T(8,128)S(1)}, f32[16,4096]{1,0:T(8,128)S(1)}, u32[]{:S(2)}, u32[]{:S(2)}) collective-permute-start(f32[16,4096]{1,0:T(8,128)S(1)} %add.49), channel_id=1, source_target_pairs={{0,2},{1,3},{2,0},{3,1},{4,6},{5,7},{6,4},{7,5},{8,10},{9,11},{10,... | collective-permute-start | bytes 786440 | tf_op jit(solution)/shard_map/ppermute | solution.py:60
  190.4 1.6 collective-permute-start.4
  191.9 8.4 %collective-permute-start.5 = (f32[16,4096]{1,0:T(8,128)S(1)}, f32[16,4096]{1,0:T(8,128)S(1)}, u32[]{:S(2)}, u32[]{:S(2)}) collective-permute-start(f32[16,4096]{1,0:T(8,128)S(1)} %add.51), channel_id=1, source_target_pairs={{0,2},{1,3},{2,0},{3,1},{4,6},{5,7},{6,4},{7,5},{8,10},{9,11},{10,... | collective-permute-start | bytes 786440 | tf_op jit(solution)/shard_map/ppermute | solution.py:60
